TPU v7x, 512 devices: a whole 4x4x16 slice. The times are simulated.
512 devices in a mesh: expert: 64 (over z, y), tensor: 8 (over x, core).
Axes of the slice: x: 4, y: 4, z: 16, core: 2. Of those that a mesh axis runs over, the one named last changes fastest.
Arguments:
- tokens: bfloat16 [32768, 1024], P('expert', 'tensor'), may hold values from -6 to 6
- expert_ids: int32 [32768], P('expert'), may hold values from 0 to 63, as said below
- gate_scale: float32 [32768], P('expert'), may hold values from 0.25 to 1
- gate_weight: bfloat16 [64, 1024, 6144], P('expert', None, 'tensor'), may hold values from -0.1875 to 0.1875
- up_weight: bfloat16 [64, 1024, 6144], P('expert', None, 'tensor'), may hold values from -0.1875 to 0.1875
- down_weight: bfloat16 [64, 6144, 1024], P('expert', 'tensor'), may hold values from -0.109375 to 0.109375
Outputs:
- combined: bfloat16 [32768, 1024], P('expert', 'tensor')
Inputs may be any that keep to these rules, and one draw needn't show every extreme that they name: `expert_ids`: among the 512 tokens of one index of expert, no expert id appears more than 16 times, and one expert, the same for every index, appears exactly 16 times in each.
All inputs are finite; a program needn't handle non-finite values.
Results may differ from a plain program's by a relative error of at most 0.02.
Values may be sent and summed in bfloat16 or wider, within the bound.
A program may use at most 64 MiB of HBM per device.

v0:
```python
import jax
import jax.numpy as jnp
from jax import lax
from jax.sharding import PartitionSpec as P


def slot_targets(expert_ids, n_expert, capacity):
    owners = jnp.arange(n_expert, dtype=jnp.int32)
    onehot = (expert_ids[:, None] == owners[None, :]).astype(jnp.int32)
    earlier = jnp.cumsum(onehot, axis=0) - onehot
    slot_rank = jnp.sum(earlier * onehot, axis=1)
    return expert_ids * capacity + slot_rank


def shards(tokens, expert_ids, gate_scale, gate_weight, up_weight, down_weight):
    n_expert = lax.axis_size("expert")
    tok_dev = tokens.shape[0]
    capacity = 2 * tok_dev // n_expert
    slot_count = n_expert * capacity
    targets = slot_targets(expert_ids, n_expert, capacity)
    w_gate = gate_weight[0]
    w_up = up_weight[0]
    w_down = down_weight[0]
    outgoing = jnp.zeros((slot_count, tokens.shape[1]), jnp.bfloat16).at[targets].set(tokens)
    arrived = lax.all_to_all(
        outgoing.reshape(n_expert, capacity, -1), "expert", split_axis=0, concat_axis=0, tiled=True
    )
    arrived = arrived.reshape(slot_count, -1)
    piece = lax.all_gather(arrived, "tensor", axis=1, tiled=True)
    gate = jnp.dot(piece, w_gate, preferred_element_type=jnp.float32)
    up = jnp.dot(piece, w_up, preferred_element_type=jnp.float32)
    hidden = (jax.nn.silu(gate) * up).astype(jnp.bfloat16)
    partial_value = jnp.dot(hidden, w_down, preferred_element_type=jnp.float32)
    summed = lax.psum_scatter(
        partial_value.astype(jnp.bfloat16), "tensor", scatter_dimension=1, tiled=True
    )
    returned = lax.all_to_all(
        summed.reshape(n_expert, capacity, -1), "expert", split_axis=0, concat_axis=0, tiled=True
    )
    returned = returned.reshape(slot_count, -1)
    picked = returned[targets]
    return (gate_scale[:, None] * picked.astype(jnp.float32)).astype(jnp.bfloat16)


def solution(mesh):
    in_specs = (
        P("expert", "tensor"),
        P("expert"),
        P("expert"),
        P("expert", None, "tensor"),
        P("expert", None, "tensor"),
        P("expert", "tensor", None),
    )
    out_specs = P("expert", "tensor")
    return jax.shard_map(shards, mesh=mesh, in_specs=in_specs, out_specs=out_specs, check_vma=False)
```

profile of v0, /device:TPU:7, one launch (start us, length us, event | category | flops | bytes accessed | tf_op | source)
XLA Modules:
  0.0 185.8 jit_solution(13820886804423058467)
XLA Ops:
  6.5 0.0 copy-start
  6.5 0.0 all-gather.2.cloned.1.call-start
  6.5 0.8 fusion.11
  7.4 1.2 reduce-window.6
  8.6 0.2 slice_reduce_fusion
  8.8 0.8 fusion.8
  9.6 0.7 compare_select_fusion
  10.3 2.2 %scatter_custom_fusion = bf16[1024,128]{1,0:T(8,128)(2,1)S(1)} fusion(s32[512]{0:T(512)S(1)} %compare_select_fusion, bf16[512,128]{1,0:T(8,128)(2,1)} %param.6, bf16[]{:T(256)} %constant.5.clone.1), kind=kCustom, calls=%fused_computation.17 | custom fusion | bytes 262656 | tf_op jit(solution)/shard_map/scatter | solution.py:24
  12.5 37.6 %all_to_all.10 = bf16[64,16,128]{2,1,0:T(8,128)(2,1)} all-to-all(bf16[64,16,128]{2,1,0:T(8,128)(2,1)S(1)} %bitcast.42), channel_id=1, replica_groups=mesh['expert'=64,'tensor'=8] {'expert'}, dimensions={0} | all-to-all | bytes 524288 | tf_op jit(solution)/shard_map/all_to_all | solution.py:25
  50.1 0.0 all-gather.2.cloned.1.call-update
  50.1 0.0 copy-start.2
  50.1 0.0 reduce-scatter.4.cloned.1.call-start
  50.2 28.9 %all-gather.2.cloned.1.call-done = bf16[1024,1024]{1,0:T(8,128)(2,1)} async-done(((bf16[1024,128]{1,0:T(8,128)(2,1)}), bf16[1024,1024]{1,0:T(8,128)(2,1)}) %all-gather.2.cloned.1.call-update) | async-done | bytes 2097168 | tf_op jit(solution)/shard_map/all_gather | solution.py:29
  79.1 5.5 %fusion.2 = f32[1024,768]{1,0:T(8,128)} fusion(bf16[1024,1024]{1,0:T(8,128)(2,1)} %all-gather.2.cloned.1.call-done, bf16[1,1024,768]{2,1,0:T(8,128)(2,1)} %param.9), kind=kOutput, calls=%fused_computation.6 | convolution fusion | flops 1610612736 | bytes 6815744 | tf_op jit(solution)/shard_map/dot_general | solution.py:30
  84.6 0.0 copy-done
  84.6 8.3 %convolution_convert_fusion = bf16[1024,1024]{1,0:T(8,128)(2,1)} fusion(bf16[1,768,1024]{2,1,0:T(8,128)(2,1)S(1)} %copy-done, f32[1024,768]{1,0:T(8,128)} %fusion.2, bf16[1024,1024]{1,0:T(8,128)(2,1)} %all-gather.2.cloned.1.call-done, bf16[1,1024,768]{2,1,0:T(8,128)(2,1)S(1)} %copy-done.2), kind=kOutput, calls=%fused_computation.3 | convolution fusion | flops 3226992640 | bytes 10485760 | tf_op jit(solution)/shard_map/dot_general | solution.py:33
  92.9 4.0 %copy.9 = bf16[1024,1024]{0,1:T(8,128)(2,1)} copy(bf16[1024,1024]{1,0:T(8,128)(2,1)} %convolution_convert_fusion) | data formatting | bytes 4194304
  96.8 0.0 reduce-scatter.4.cloned.1.call-update
  96.8 42.0 %reduce-scatter.4.cloned.1.call-done = bf16[128,1024]{1,0:T(8,128)(2,1)} async-done(((bf16[1024,1024]{1,0:T(8,128)(2,1)}), bf16[128,1024]{1,0:T(8,128)(2,1)}) %reduce-scatter.4.cloned.1.call-update) | async-done | bytes 262160
  138.8 1.8 copy.10
  140.6 14.4 %all-to-all-start.1 = ((bf16[64,16,128]{2,1,0:T(8,128)(2,1)}), bf16[64,16,128]{2,1,0:T(8,128)(2,1)S(1)}, u32[]{:S(2)}, u32[]{:S(2)}) async-start(bf16[64,16,128]{2,1,0:T(8,128)(2,1)} %bitcast.7), calls=%async_computation.1 | async-start | bytes 524288 | tf_op jit(solution)/shard_map/all_to_all | solution.py:37
  155.0 21.8 %all-to-all-done.1 = bf16[64,16,128]{2,1,0:T(8,128)(2,1)S(1)} async-done(((bf16[64,16,128]{2,1,0:T(8,128)(2,1)}), bf16[64,16,128]{2,1,0:T(8,128)(2,1)S(1)}, u32[]{:S(2)}, u32[]{:S(2)}) %all-to-all-start.1) | async-done | bytes 262176 | tf_op jit(solution)/shard_map/all_to_all | solution.py:37
  176.8 1.3 gather_fusion
  178.1 0.8 multiply_convert_fusion.1
  (6 shorter events, 0.1 us)
Async XLA Ops:
  6.5 78.1 %copy-start = (bf16[1,768,1024]{2,1,0:T(8,128)(2,1)S(1)}, bf16[1,768,1024]{2,1,0:T(8,128)(2,1)}, u32[]{:S(2)}) copy-start(bf16[1,768,1024]{2,1,0:T(8,128)(2,1)} %param.11) | copy-start | bytes 4718596
  6.5 72.6 %all-gather.2.cloned.1.call-start = ((), (), s32[]{:S(2)}) async-start(), calls=%async_computation.3 | async-start | bytes 2359296 | tf_op jit(solution)/shard_map/all_gather | solution.py:29
  50.1 34.5 %copy-start.2 = (bf16[1,1024,768]{2,1,0:T(8,128)(2,1)S(1)}, bf16[1,1024,768]{2,1,0:T(8,128)(2,1)}, u32[]{:S(2)}) copy-start(bf16[1,1024,768]{2,1,0:T(8,128)(2,1)} %param.10) | copy-start | bytes 4718596
  50.1 88.7 %reduce-scatter.4.cloned.1.call-start = ((), (), s32[]{:S(2)}) async-start(), calls=%async_computation.4 | async-start | bytes 2359296
  96.8 81.3 %copy-start.1 = (f32[512]{0:T(512)S(1)}, f32[512]{0:T(512)}, u32[]{:S(2)}) copy-start(f32[512]{0:T(512)} %param.8) | copy-start | bytes 6148
  140.6 36.2 %all-to-all-start.1 = ((bf16[64,16,128]{2,1,0:T(8,128)(2,1)}), bf16[64,16,128]{2,1,0:T(8,128)(2,1)S(1)}, u32[]{:S(2)}, u32[]{:S(2)}) async-start(bf16[64,16,128]{2,1,0:T(8,128)(2,1)} %bitcast.7), calls=%async_computation.1 | async-start | bytes 524288 | tf_op jit(solution)/shard_map/all_to_all | solution.py:37
Sparse Core Ops, SparseCore 0:
  50.2 28.8 all-gather.1
  96.9 41.8 reduce-scatter.3
where the time goes:
time: 186 us
  waiting for transfers between devices  92.7 us (50%)
  blocking collectives  37.6 us (20%)
  starting transfers between devices  14.4 us (8%)
  matrix products  13.7 us (7%)
  between operations  13.5 us (7%)
  local copies, waits for them, and re-layouts  9.49 us (5%)
  other arithmetic  4.34 us (2%)
    unnamed x3, waiting for transfers between devices  42 us
    all_to_all x1, blocking collectives, shards(): lax.all_to_all(outgoing.reshape(n_expert, capacity, -1), 'expert', split_...  37.6 us
    all_gather x1, waiting for transfers between devices, shards(): piece = lax.all_gather(arrived, 'tensor', axis=1, tiled=True)  28.9 us
    all_to_all x1, waiting for transfers between devices, shards(): lax.all_to_all(summed.reshape(n_expert, capacity, -1), 'expert', split_ax...  21.8 us
    all_to_all x1, starting transfers between devices, shards(): lax.all_to_all(summed.reshape(n_expert, capacity, -1), 'expert', split_ax...  14.4 us
    dot_general x1, matrix products, shards(): partial_value = jnp.dot(hidden, w_down, preferred_element_type=jnp.float32)  8.25 us
    unnamed x8, local copies, waits for them, and re-layouts  5.74 us
    dot_general x1, matrix products, shards(): gate = jnp.dot(piece, w_gate, preferred_element_type=jnp.float32)  5.49 us
  transfers between devices with their start and end apart: 3, of which 3 were waited for; matrix products, arithmetic and copies ran while one was open for 0% of the time, Pallas kernels for 0%

commit v1 on v0

v1 whole, which is shorter than its diff:
```python
import jax
import jax.numpy as jnp
from jax import lax
from jax.experimental import pallas as pl
from jax.experimental.pallas import tpu as pltpu
from jax.sharding import PartitionSpec as P

NZ, NY, NX, NC = 16, 4, 4, 2
CHUNKS, PER = 4, 4
CAP = 16
TOK = 512
D = 1024
FEAT = 128
WIDE = 256
HID = 768
ROWS = PER * 2 * CAP
DZ = (8, 0, 4, -4, 7, -6, -2, 1, -7, 6, 2, -1, 5, -5, 3, -3)
BF = jnp.bfloat16
F32 = jnp.float32


def dev(z, y, x, c):
    return {"expert": z * NY + y, "tensor": x * NC + c}


def rcopy(src, dst, send, recv, target):
    return pltpu.make_async_remote_copy(
        src_ref=src, dst_ref=dst, send_sem=send, recv_sem=recv,
        device_id=target, device_id_type=pl.DeviceIdType.MESH,
    )


def kernel(ids_ref, scale_ref, tok_ref, wg_hbm, wu_hbm, wd_hbm, out_ref,
           outg, mid, xbuf, ybuf, rsbuf, zbuf, mid2, ret, pick, scol, wg, wu, wd,
           w_sem, ws_send, ws_recv, y_send, y_self, y_recv, z_send, z_recv, ag_send, ag_recv,
           rs_send, rs_recv, zr_send, zr_recv, yr_send, yr_recv):
    e = lax.axis_index("expert")
    t = lax.axis_index("tensor")
    z, y, x, c = e // NY, e % NY, t // NC, t % NC
    half, within = y // 2, y % 2
    cols = pl.ds(pl.multiple_of(x * WIDE, WIDE), WIDE)
    my_cols = pl.ds(pl.multiple_of(c * FEAT, FEAT), FEAT)

    barrier = pltpu.get_barrier_semaphore()
    peers = [dev((z + d) % NZ, y, x, c) for d in (8, 7, 9, 6, 10, 5, 11, 4, 12, 3, 13, 2, 14, 1, 15)]
    peers += [dev(z, (y + d) % NY, x, cc) for d in (2, 1, 3) for cc in (0, 1)]
    peers += [dev(z, y, (x + d) % NX, c) for d in (2, 1, 3)] + [dev(z, y, x, 1 - c)]
    for peer in peers:
        pl.semaphore_signal(barrier, inc=1, device_id=peer, device_id_type=pl.DeviceIdType.MESH)

    weights = ((wg_hbm, wg), (wu_hbm, wu), (wd_hbm, wd))
    own = [pltpu.make_async_copy(hbm, buf.at[0], w_sem.at[n]) for n, (hbm, buf) in enumerate(weights)]
    for copy in own:
        copy.start()

    row = lax.broadcasted_iota(jnp.int32, (64, TOK), 0)
    place = (row >> 4) * PER + (row & 3)
    dz = jnp.zeros_like(row)
    for i, d in enumerate(DZ):
        dz = jnp.where(place == i, d, dz)
    owner = ((z - dz) & (NZ - 1)) * NY + ((row >> 2) & 3)
    hot = owner == ids_ref[...]
    before = (lax.broadcasted_iota(jnp.int32, (TOK, TOK), 0)
              < lax.broadcasted_iota(jnp.int32, (TOK, TOK), 1)).astype(F32).astype(BF)
    earlier = jnp.dot(hot.astype(F32).astype(BF), before, preferred_element_type=F32)
    slot = jnp.sum(jnp.where(hot, earlier + (row * CAP).astype(F32), 0.0), axis=0, keepdims=True)
    slot_i = slot.astype(jnp.int32)
    for k in range(CHUNKS):
        rows = lax.broadcasted_iota(jnp.int32, (256, TOK), 0) + k * 256
        sel = (rows == slot_i).astype(F32).astype(BF)
        part = jnp.dot(sel, tok_ref[...], preferred_element_type=F32).astype(BF)
        outg[k] = part.reshape(NY, PER, CAP, FEAT)

    pl.semaphore_wait(barrier, len(peers))

    def along_y(k):
        for d in (2, 1, 3):
            yy = (y + d) % NY
            rcopy(outg.at[k, yy], mid.at[pl.ds(k * PER, PER), within, :, my_cols],
                  y_send, y_recv.at[k], dev(z, yy, x, half)).start()
        src = outg.at[k, y]
        dst = mid.at[pl.ds(k * PER, PER), within, :, my_cols]

        @pl.when(c == half)
        def _():
            pltpu.make_async_copy(src, dst, y_recv.at[k]).start()

        @pl.when(c != half)
        def _():
            rcopy(src, dst, y_self, y_recv.at[k], dev(z, y, x, 1 - c)).start()

    for k in range(CHUNKS):
        along_y(k)
    sib = dev(z, y, x, 1 - c)
    swap = [rcopy(hbm, buf.at[1], ws_send.at[n], ws_recv.at[n], sib) for n, (hbm, buf) in enumerate(weights)]
    for copy in swap:
        copy.start()

    for k in range(CHUNKS):
        whole = mid.at[pl.ds(k * PER, PER)]
        pltpu.make_async_copy(whole, whole, y_recv.at[k]).wait()
        for i in range(k * PER, (k + 1) * PER):
            dst = xbuf.at[i, :, :, cols]
            if DZ[i] == 0:
                pltpu.make_async_copy(mid.at[i], dst, z_recv.at[k]).start()
            else:
                rcopy(mid.at[i], dst, z_send, z_recv.at[k], dev((z - DZ[i]) % NZ, y, x, c)).start()

    slot_col = jnp.broadcast_to(slot, (128, TOK)).T.astype(jnp.int32)
    scol[...] = jnp.broadcast_to(scale_ref[...], (128, TOK)).T
    for n in range(8):
        lanes = lax.broadcasted_iota(jnp.int32, (TOK, 128), 1) + n * 128
        pick[:, n * 128:(n + 1) * 128] = (lanes == slot_col).astype(F32).astype(BF)

    def gather(k):
        part = xbuf.at[pl.ds(k * PER, PER), :, :, cols]
        pltpu.make_async_copy(part, part, z_recv.at[k]).wait()
        for d in (2, 1, 3):
            rcopy(part, part, ag_send, ag_recv.at[k], dev(z, y, (x + d) % NX, c)).start()

    def ffn(k):
        three = xbuf.at[pl.ds(k * PER, PER), :, :, pl.ds(0, 3 * WIDE)]
        pltpu.make_async_copy(three, three, ag_recv.at[k]).wait()
        rows = xbuf[k * PER:(k + 1) * PER].reshape(ROWS, D)
        total = None
        for s in range(2):
            if k == 0:
                if s == 0:
                    for copy in own:
                        copy.wait()
                else:
                    for copy in swap:
                        copy.wait()
            gate = jnp.dot(rows, wg[s], preferred_element_type=F32)
            up = jnp.dot(rows, wu[s], preferred_element_type=F32)
            hidden = (gate / (1.0 + jnp.exp(-gate)) * up).astype(BF)
            part = jnp.dot(hidden, wd[s], preferred_element_type=F32)
            total = part if total is None else total + part
        total = total.astype(BF)
        for n in range(NX):
            ybuf[n, k] = total[:, n * WIDE:(n + 1) * WIDE]
        for d in (2, 1, 3):
            xx = (x + d) % NX
            rcopy(ybuf.at[xx, k], rsbuf.at[k, d - 1], rs_send, rs_recv.at[k], dev(z, y, xx, c)).start()

    def back_z(k):
        three = rsbuf.at[k]
        pltpu.make_async_copy(three, three, rs_recv.at[k]).wait()
        total = ybuf[x, k].astype(F32)
        for n in range(3):
            total += rsbuf[k, n].astype(F32)
        zbuf[k * PER:(k + 1) * PER] = total.astype(BF).reshape(PER, 2, CAP, WIDE)
        for i in range(k * PER, (k + 1) * PER):
            if DZ[i] == 0:
                pltpu.make_async_copy(zbuf.at[i], mid2.at[i], zr_recv.at[k]).start()
            else:
                rcopy(zbuf.at[i], mid2.at[i], zr_send, zr_recv.at[k], dev((z + DZ[i]) % NZ, y, x, c)).start()

    def back_y(k):
        whole = mid2.at[pl.ds(k * PER, PER)]
        pltpu.make_async_copy(whole, whole, zr_recv.at[k]).wait()
        for s in range(2):
            for cc in range(NC):
                src = mid2.at[pl.ds(k * PER, PER), s, :, pl.ds(cc * FEAT, FEAT)]
                yy = 2 * c + s
                mine = jnp.logical_and(yy == y, c == cc)

                @pl.when(mine)
                def _():
                    pltpu.make_async_copy(src, ret.at[k, y], yr_recv.at[k]).start()

                @pl.when(jnp.logical_not(mine))
                def _():
                    rcopy(src, ret.at[k, y], yr_send, yr_recv.at[k], dev(z, yy, x, cc)).start()

    def combine(k):
        whole = ret.at[k]
        pltpu.make_async_copy(whole, whole, yr_recv.at[k]).wait()
        return jnp.dot(pick[:, k * 256:(k + 1) * 256], ret[k].reshape(256, FEAT), preferred_element_type=F32)

    gather(0)
    gather(1)
    ffn(0)
    gather(2)
    ffn(1)
    back_z(0)
    gather(3)
    ffn(2)
    back_z(1)
    back_y(0)
    ffn(3)
    back_z(2)
    back_y(1)
    back_z(3)
    back_y(2)
    back_y(3)
    picked = combine(0)
    for k in range(1, CHUNKS):
        picked += combine(k)
    out_ref[...] = (scol[...] * picked).astype(BF)

    def sent(ref, sem):
        pltpu.make_async_copy(ref, ref, sem).wait()

    sent(outg.at[:, pl.ds(0, 3)], y_send)

    @pl.when(c != half)
    def _():
        sent(outg.at[:, 0], y_self)

    sent(mid.at[pl.ds(0, NZ - 1)], z_send)
    sent(xbuf.at[:, :, :, pl.ds(0, 3 * WIDE)], ag_send)
    sent(ybuf.at[pl.ds(0, 3)], rs_send)
    sent(zbuf.at[pl.ds(0, NZ - 1)], zr_send)

    @pl.when(c == half)
    def _():
        sent(ret.at[:, pl.ds(0, 3)], yr_send)

    @pl.when(c != half)
    def _():
        sent(ret, yr_send)


def shards(tokens, expert_ids, gate_scale, gate_weight, up_weight, down_weight):
    vmem = pl.BlockSpec(memory_space=pltpu.VMEM)
    hbm = pl.BlockSpec(memory_space=pl.ANY)
    dma = pltpu.SemaphoreType.DMA
    return pl.pallas_call(
        kernel,
        out_shape=jax.ShapeDtypeStruct((TOK, FEAT), BF),
        in_specs=[vmem, vmem, vmem, hbm, hbm, hbm],
        out_specs=vmem,
        scratch_shapes=[
            pltpu.VMEM((CHUNKS, NY, PER, CAP, FEAT), BF),
            pltpu.VMEM((NZ, 2, CAP, WIDE), BF),
            pltpu.VMEM((NZ, 2, CAP, D), BF),
            pltpu.VMEM((NX, CHUNKS, ROWS, WIDE), BF),
            pltpu.VMEM((CHUNKS, 3, ROWS, WIDE), BF),
            pltpu.VMEM((NZ, 2, CAP, WIDE), BF),
            pltpu.VMEM((NZ, 2, CAP, WIDE), BF),
            pltpu.VMEM((CHUNKS, NY, PER, CAP, FEAT), BF),
            pltpu.VMEM((TOK, CHUNKS * 256), BF),
            pltpu.VMEM((TOK, FEAT), F32),
            pltpu.VMEM((2, D, HID), BF),
            pltpu.VMEM((2, D, HID), BF),
            pltpu.VMEM((2, HID, D), BF),
            dma((3,)), dma((3,)), dma((3,)),
            dma, dma, dma((CHUNKS,)),
            dma, dma((CHUNKS,)),
            dma, dma((CHUNKS,)),
            dma, dma((CHUNKS,)),
            dma, dma((CHUNKS,)),
            dma, dma((CHUNKS,)),
        ],
        compiler_params=pltpu.CompilerParams(
            collective_id=0, has_side_effects=True, vmem_limit_bytes=56 << 20
        ),
        name="moe",
    )(expert_ids.reshape(1, TOK), gate_scale.reshape(1, TOK), tokens, gate_weight[0], up_weight[0], down_weight[0])


def solution(mesh):
    in_specs = (
        P("expert", "tensor"),
        P("expert"),
        P("expert"),
        P("expert", None, "tensor"),
        P("expert", None, "tensor"),
        P("expert", "tensor", None),
    )
    out_specs = P("expert", "tensor")
    return jax.shard_map(shards, mesh=mesh, in_specs=in_specs, out_specs=out_specs, check_vma=False)
```

time: 186 us -> 70 us (0.38)
  the two profiles are of different devices: /device:TPU:7 before, /device:TPU:1 now
where the time goes in v1:
time: 70 us; the launch traced here: 69.9 us
  Pallas kernels  68.3 us (98%)
  local copies, waits for them, and re-layouts  1.57 us (2%)
    pallas_call x1, Pallas kernels, shards(): pl.pallas_call(kernel, out_shape=jax.ShapeDtypeStruct((TOK, FEAT), BF), i...  68.3 us
    unnamed x1, local copies, waits for them, and re-layouts  1.57 us

profile of v1, /device:TPU:1, one launch (start us, length us, event | category | flops | bytes accessed | tf_op | source)
XLA Modules:
  0.0 69.9 jit_solution(4348762588932882937)
XLA Ops:
  0.0 68.3 %moe.1 = bf16[512,128]{1,0:T(8,128)(2,1)} custom-call(s32[1,512]{1,0:T(1,128)} %bitcast.8, f32[1,512]{1,0:T(1,128)} %bitcast.9, bf16[512,128]{1,0:T(8,128)(2,1)} %tok_ref.1, bf16[1024,768]{1,0:T(8,128)(2,1)} %bitcast.5, bf16[1024,768]{1,0:T(8,128)(2,1)} %bitcast.6, bf16[768,1024]{1,0:T(8,128)(2,1)} %bitcast.7), custom_call_target="tpu_custom_call" | custom-call | tf_op jit(solution)/shard_map/moe/pallas_call | solution.py:229
  68.3 1.6 %copy.8 = bf16[512,128]{1,0:T(8,128)(2,1)} copy(bf16[512,128]{1,0:T(8,128)(2,1)} %moe.1) | data formatting | bytes 262144

commit v2 on v0

v2 whole, which is shorter than its diff:
```python
import jax
import jax.numpy as jnp
from jax import lax
from jax.experimental import pallas as pl
from jax.experimental.pallas import tpu as pltpu
from jax.sharding import PartitionSpec as P

NZ, NY, NX, NC = 16, 4, 4, 2
CHUNKS = 8
PER = 2
CAP = 16
TOK = 512
D = 1024
FEAT = 128
WIDE = 256
HID = 768
ROWS = PER * 2 * CAP
SLOTS = PER * NY * CAP
DZ = (8, 7, -7, 6, -6, 5, -5, 4, -4, 3, -3, 2, 0, 1, -1, -2)
ISSUE = tuple(range(CHUNKS))
BF = jnp.bfloat16
F32 = jnp.float32
MESH = pl.DeviceIdType.MESH


def wrap(a, n):
    return lax.rem(a, n)


def dev(z, y, x, c):
    return {"expert": z * NY + y, "tensor": x * NC + c}


def rcopy(src, dst, send, recv, target):
    return pltpu.make_async_remote_copy(
        src_ref=src, dst_ref=dst, send_sem=send, recv_sem=recv, device_id=target, device_id_type=MESH
    )


def done(ref, sem):
    pltpu.make_async_copy(ref, ref, sem).wait()


def kernel(ids_ref, tok_ref, wg_hbm, wu_hbm, wd_hbm, out_ref,
           outg, arr, xbuf, ybuf, rsbuf, zbuf, ret, pick, wg, wu, wd,
           w_sem, ws_send, ws_recv, d_send, d_recv, ag_send, ag_recv, rs_send, rs_recv, rt_send, rt_recv):
    e = lax.axis_index("expert")
    t = lax.axis_index("tensor")
    z, y = lax.div(e, NY), lax.rem(e, NY)
    x, c = lax.div(t, NC), lax.rem(t, NC)
    o = 1 - c
    right, left, far = wrap(x + 1, NX), wrap(x + 3, NX), wrap(x + 2, NX)
    ys = [y] + [wrap(y + d, NY) for d in (1, 2, 3)]

    def at_z(d):
        return wrap(z + (d + NZ), NZ) if d else z

    my_cols = pl.ds(pl.multiple_of(t * FEAT, FEAT), FEAT)

    barrier = pltpu.get_barrier_semaphore()
    peers = [(dz, dy) for dz in (8, 7, -7, 6, -6, 5, -5, 4, -4, 3, -3, 2, -2, 1, -1, 0) for dy in range(4)]
    peers = [dev(at_z(dz), ys[dy], x, c) for dz, dy in peers if (dz, dy) != (0, 0)]
    peers += [dev(z, y, xx, cc) for xx in (far, right, left) for cc in (0, 1)] + [dev(z, y, x, o)]
    for peer in peers:
        pl.semaphore_signal(barrier, inc=1, device_id=peer, device_id_type=MESH)

    weights = ((wg_hbm, wg), (wu_hbm, wu), (wd_hbm, wd))
    own = [pltpu.make_async_copy(hbm, buf.at[0], w_sem.at[n]) for n, (hbm, buf) in enumerate(weights)]
    for copy in own:
        copy.start()

    row = lax.broadcasted_iota(jnp.int32, (64, 128), 0)
    dz = jnp.zeros_like(row)
    for i, d in enumerate(DZ):
        dz = jnp.where((row >> 2) == i, d, dz)
    owner = ((z - dz) & (NZ - 1)) * NY + (row & 3)
    hot = jnp.concatenate([owner] * 4, axis=1) == ids_ref[...]
    before = (lax.broadcasted_iota(jnp.int32, (TOK, TOK), 0)
              < lax.broadcasted_iota(jnp.int32, (TOK, TOK), 1)).astype(F32).astype(BF)
    earlier = jnp.dot(hot.astype(F32).astype(BF), before, preferred_element_type=F32)
    base = lax.broadcasted_iota(jnp.int32, (64, TOK), 0).astype(F32) * float(CAP)
    slot = jnp.sum(jnp.where(hot, earlier + base, 0.0), axis=0, keepdims=True)
    slot_i = slot.astype(jnp.int32)
    for k in range(CHUNKS):
        rows = lax.broadcasted_iota(jnp.int32, (SLOTS, TOK), 0) + k * SLOTS
        sel = (rows == slot_i).astype(F32).astype(BF)
        part = jnp.dot(sel, tok_ref[...], preferred_element_type=F32).astype(BF)
        outg[k * PER:(k + 1) * PER] = part.reshape(PER, NY, CAP, FEAT)

    pl.semaphore_wait(barrier, len(peers))

    for k in ISSUE:
        for i in range(k * PER, (k + 1) * PER):
            for n, yy in enumerate(ys):
                if DZ[i] == 0 and n == 0:
                    pltpu.make_async_copy(outg.at[i, yy], arr.at[i, y], d_recv.at[k]).start()
                else:
                    rcopy(outg.at[i, yy], arr.at[i, y], d_send, d_recv.at[k], dev(at_z(-DZ[i]), yy, x, c)).start()
    sib = dev(z, y, x, o)
    swap = [rcopy(hbm, buf.at[1], ws_send.at[n], ws_recv.at[n], sib) for n, (hbm, buf) in enumerate(weights)]
    for copy in swap:
        copy.start()

    slot_col = jnp.broadcast_to(slot, (128, TOK)).T.astype(jnp.int32)
    for n in range(8):
        lanes = lax.broadcasted_iota(jnp.int32, (TOK, 128), 1) + n * 128
        pick[:, n * 128:(n + 1) * 128] = (lanes == slot_col).astype(F32).astype(BF)

    def places(k):
        return pl.ds(k * PER, PER)

    def gather(k):
        done(arr.at[places(k)], d_recv.at[k])
        for xx in (far, right, left):
            for h in range(2):
                rcopy(arr.at[places(k), pl.ds(2 * h, 2)], xbuf.at[places(k), :, :, my_cols],
                      ag_send.at[k], ag_recv.at[k], dev(z, y, xx, h)).start()
        rcopy(arr.at[places(k), pl.ds(2 * o, 2)], xbuf.at[places(k), :, :, my_cols],
              ag_send.at[k], ag_recv.at[k], sib).start()
        pltpu.make_async_copy(arr.at[places(k), pl.ds(2 * c, 2)], xbuf.at[places(k), :, :, my_cols],
                              ag_recv.at[k]).start()

    def ffn(k):
        done(xbuf.at[places(k)], ag_recv.at[k])
        rows = xbuf[k * PER:(k + 1) * PER].reshape(ROWS, D)
        total = None
        for s in range(2):
            if k == 0:
                for copy in (own, swap)[s]:
                    copy.wait()
            gate = jnp.dot(rows, wg[s], preferred_element_type=F32)
            up = jnp.dot(rows, wu[s], preferred_element_type=F32)
            hidden = (gate / (1.0 + jnp.exp(-gate)) * up).astype(BF)
            part = jnp.dot(hidden, wd[s], preferred_element_type=F32)
            total = part if total is None else total + part
        total = total.astype(BF)
        for n in range(NX * NC):
            ybuf[n, k] = total[:, n * FEAT:(n + 1) * FEAT]
        for side, target in enumerate((right, left, far)):
            for cc in range(NC):
                rcopy(ybuf.at[NC * target + cc, k], rsbuf.at[k, 4 * c + side],
                      rs_send.at[k], rs_recv.at[k], dev(z, y, target, cc)).start()
        rcopy(ybuf.at[NC * x + o, k], rsbuf.at[k, 4 * c + 3], rs_send.at[k], rs_recv.at[k], sib).start()
        rsbuf[k, 4 * c + 3] = ybuf[t, k]

    def back(k):
        done(rsbuf.at[k, pl.ds(0, 7)], rs_recv.at[k])
        for h in range(2):
            total = rsbuf[k, 4 * h + 3].astype(F32)
            for n in range(3):
                total += rsbuf[k, 4 * h + n].astype(F32)
            zbuf[k * PER:(k + 1) * PER, 2 * h:2 * h + 2] = total.astype(BF).reshape(PER, 2, CAP, FEAT)
        for i in range(k * PER, (k + 1) * PER):
            for n, yy in enumerate(ys):
                if DZ[i] == 0 and n == 0:
                    pltpu.make_async_copy(zbuf.at[i, yy], ret.at[i, y], rt_recv.at[k]).start()
                else:
                    rcopy(zbuf.at[i, yy], ret.at[i, y], rt_send, rt_recv.at[k], dev(at_z(DZ[i]), yy, x, c)).start()

    def combine(k):
        done(ret.at[places(k)], rt_recv.at[k])
        return jnp.dot(pick[:, k * SLOTS:(k + 1) * SLOTS], ret[k * PER:(k + 1) * PER].reshape(SLOTS, FEAT),
                       preferred_element_type=F32)

    gather(0)
    gather(1)
    gather(2)
    gather(3)
    ffn(0)
    gather(4)
    ffn(1)
    gather(5)
    ffn(2)
    gather(6)
    ffn(3)
    back(0)
    gather(7)
    ffn(4)
    back(1)
    ffn(5)
    back(2)
    ffn(6)
    back(3)
    ffn(7)
    back(4)
    back(5)
    back(6)
    back(7)
    picked = combine(0)
    for k in range(1, CHUNKS):
        picked += combine(k)
    out_ref[...] = picked.astype(BF)

    blocks = wg.at[0, pl.ds(0, 63 * CAP), pl.ds(0, FEAT)]
    done(blocks, d_send)
    for k in range(CHUNKS):
        done(rsbuf.at[k, pl.ds(0, 7)], ag_send.at[k])
        done(rsbuf.at[k, pl.ds(0, 7)], rs_send.at[k])
    done(blocks, rt_send)


def shards(tokens, expert_ids, gate_scale, gate_weight, up_weight, down_weight):
    vmem = pl.BlockSpec(memory_space=pltpu.VMEM)
    hbm = pl.BlockSpec(memory_space=pl.ANY)
    dma = pltpu.SemaphoreType.DMA
    picked = pl.pallas_call(
        kernel,
        out_shape=jax.ShapeDtypeStruct((TOK, FEAT), BF),
        in_specs=[vmem, vmem, hbm, hbm, hbm],
        out_specs=vmem,
        scratch_shapes=[
            pltpu.VMEM((NZ, NY, CAP, FEAT), BF),
            pltpu.VMEM((NZ, NY, CAP, FEAT), BF),
            pltpu.VMEM((NZ, 2, CAP, D), BF),
            pltpu.VMEM((NX * NC, CHUNKS, ROWS, FEAT), BF),
            pltpu.VMEM((CHUNKS, 8, ROWS, FEAT), BF),
            pltpu.VMEM((NZ, NY, CAP, FEAT), BF),
            pltpu.VMEM((NZ, NY, CAP, FEAT), BF),
            pltpu.VMEM((TOK, CHUNKS * SLOTS), BF),
            pltpu.VMEM((2, D, HID), BF),
            pltpu.VMEM((2, D, HID), BF),
            pltpu.VMEM((2, HID, D), BF),
            dma((3,)), dma((3,)), dma((3,)),
            dma, dma((CHUNKS,)),
            dma((CHUNKS,)), dma((CHUNKS,)),
            dma((CHUNKS,)), dma((CHUNKS,)),
            dma, dma((CHUNKS,)),
        ],
        compiler_params=pltpu.CompilerParams(
            collective_id=0, has_side_effects=True, vmem_limit_bytes=56 << 20
        ),
        name="moe",
    )(expert_ids.reshape(1, TOK), tokens, gate_weight[0], up_weight[0], down_weight[0])
    return (gate_scale[:, None] * picked.astype(F32)).astype(BF)


def solution(mesh):
    in_specs = (
        P("expert", "tensor"),
        P("expert"),
        P("expert"),
        P("expert", None, "tensor"),
        P("expert", None, "tensor"),
        P("expert", "tensor", None),
    )
    out_specs = P("expert", "tensor")
    return jax.shard_map(shards, mesh=mesh, in_specs=in_specs, out_specs=out_specs, check_vma=False)
```

time: 186 us -> 63.8 us (0.34)
  the two profiles are of different devices: /device:TPU:7 before, /device:TPU:1 now
where the time goes in v2:
time: 63.8 us; the launch traced here: 63.7 us
  Pallas kernels  62 us (97%)
  other arithmetic  1.7 us (3%)
    pallas_call x1, Pallas kernels, shards(): pl.pallas_call(kernel, out_shape=jax.ShapeDtypeStruct((TOK, FEAT), BF), i...  62 us
    convert_element_type x1, other arithmetic, shards(): return (gate_scale[:, None] * picked.astype(F32)).astype(BF)  1.7 us

profile of v2, /device:TPU:1, one launch (start us, length us, event | category | flops | bytes accessed | tf_op | source)
XLA Modules:
  0.0 63.7 jit_solution(14122473248420738914)
XLA Ops:
  0.0 0.0 copy-start
  0.0 62.0 %moe.1 = bf16[512,128]{1,0:T(8,128)(2,1)} custom-call(s32[1,512]{1,0:T(1,128)} %bitcast.7, bf16[512,128]{1,0:T(8,128)(2,1)} %tok_ref.1, bf16[1024,768]{1,0:T(8,128)(2,1)} %bitcast.4, bf16[1024,768]{1,0:T(8,128)(2,1)} %bitcast.5, bf16[768,1024]{1,0:T(8,128)(2,1)} %bitcast.6), custom_call_target="tpu_custom_call" | custom-call | tf_op jit(solution)/shard_map/moe/pallas_call | solution.py:206
  62.0 0.0 copy-done
  62.0 1.7 %multiply_convert_fusion = bf16[512,128]{1,0:T(8,128)(2,1)} fusion(bf16[512,128]{1,0:T(8,128)(2,1)} %moe.1, f32[512]{0:T(512)S(1)} %copy-done), kind=kLoop, calls=%fused_computation | loop fusion | flops 196608 | bytes 264192 | tf_op jit(solution)/shard_map/convert_element_type | solution.py:234
Async XLA Ops:
  0.0 62.0 %copy-start = (f32[512]{0:T(512)S(1)}, f32[512]{0:T(512)}, u32[]{:S(2)}) copy-start(f32[512]{0:T(512)} %param.8) | copy-start | bytes 6148

commit v3 on v2

--- a/solution.py
+++ b/solution.py
@@ -16,7 +16,7 @@
 HID = 768
 ROWS = PER * 2 * CAP
 SLOTS = PER * NY * CAP
-DZ = (8, 7, -7, 6, -6, 5, -5, 4, -4, 3, -3, 2, 0, 1, -1, -2)
+DZ = (8, 0, 7, -7, 6, -6, 5, -5, 4, -4, 3, -3, 2, -2, 1, -1)
 ISSUE = tuple(range(CHUNKS))
 BF = jnp.bfloat16
 F32 = jnp.float32
@@ -50,7 +50,7 @@
     x, c = lax.div(t, NC), lax.rem(t, NC)
     o = 1 - c
     right, left, far = wrap(x + 1, NX), wrap(x + 3, NX), wrap(x + 2, NX)
-    ys = [y] + [wrap(y + d, NY) for d in (1, 2, 3)]
+    ys = [y] + [wrap(y + d, NY) for d in (2, 1, 3)]
 
     def at_z(d):
         return wrap(z + (d + NZ), NZ) if d else z
@@ -89,6 +89,11 @@
 
     pl.semaphore_wait(barrier, len(peers))
 
+    sib = dev(z, y, x, o)
+    swap = [rcopy(hbm, buf.at[1], ws_send.at[n], ws_recv.at[n], sib) for n, (hbm, buf) in enumerate(weights)]
+    for copy in swap:
+        copy.start()
+
     for k in ISSUE:
         for i in range(k * PER, (k + 1) * PER):
             for n, yy in enumerate(ys):
@@ -96,11 +101,6 @@
                     pltpu.make_async_copy(outg.at[i, yy], arr.at[i, y], d_recv.at[k]).start()
                 else:
                     rcopy(outg.at[i, yy], arr.at[i, y], d_send, d_recv.at[k], dev(at_z(-DZ[i]), yy, x, c)).start()
-    sib = dev(z, y, x, o)
-    swap = [rcopy(hbm, buf.at[1], ws_send.at[n], ws_recv.at[n], sib) for n, (hbm, buf) in enumerate(weights)]
-    for copy in swap:
-        copy.start()
-
     slot_col = jnp.broadcast_to(slot, (128, TOK)).T.astype(jnp.int32)
     for n in range(8):
         lanes = lax.broadcasted_iota(jnp.int32, (TOK, 128), 1) + n * 128
@@ -136,7 +136,7 @@
         total = total.astype(BF)
         for n in range(NX * NC):
             ybuf[n, k] = total[:, n * FEAT:(n + 1) * FEAT]
-        for side, target in enumerate((right, left, far)):
+        for side, target in ((2, far), (0, right), (1, left)):
             for cc in range(NC):
                 rcopy(ybuf.at[NC * target + cc, k], rsbuf.at[k, 4 * c + side],
                       rs_send.at[k], rs_recv.at[k], dev(z, y, target, cc)).start()

time: 63.8 us -> 62.9 us (0.986)
  Pallas kernels: 62 us -> 61 us
    pallas_call x1, Pallas kernels: 62 us -> 61 us  [shards(): pl.pallas_call(kernel, out_shape=jax.ShapeDtypeStruct((TOK, FEAT), BF), i...]
where the time goes in v3:
time: 62.9 us; the launch traced here: 62.7 us
  Pallas kernels  61 us (97%)
  other arithmetic  1.7 us (3%)
    pallas_call x1, Pallas kernels, shards(): pl.pallas_call(kernel, out_shape=jax.ShapeDtypeStruct((TOK, FEAT), BF), i...  61 us
    convert_element_type x1, other arithmetic, shards(): return (gate_scale[:, None] * picked.astype(F32)).astype(BF)  1.7 us

profile of v3, /device:TPU:1, one launch (start us, length us, event | category | flops | bytes accessed | tf_op | source)
XLA Modules:
  0.0 62.7 jit_solution(700692318941803765)
XLA Ops:
  0.0 0.0 copy-start
  0.0 61.0 %moe.1 = bf16[512,128]{1,0:T(8,128)(2,1)} custom-call(s32[1,512]{1,0:T(1,128)} %bitcast.7, bf16[512,128]{1,0:T(8,128)(2,1)} %tok_ref.1, bf16[1024,768]{1,0:T(8,128)(2,1)} %bitcast.4, bf16[1024,768]{1,0:T(8,128)(2,1)} %bitcast.5, bf16[768,1024]{1,0:T(8,128)(2,1)} %bitcast.6), custom_call_target="tpu_custom_call" | custom-call | tf_op jit(solution)/shard_map/moe/pallas_call | solution.py:206
  61.0 0.0 copy-done
  61.0 1.7 %multiply_convert_fusion = bf16[512,128]{1,0:T(8,128)(2,1)} fusion(bf16[512,128]{1,0:T(8,128)(2,1)} %moe.1, f32[512]{0:T(512)S(1)} %copy-done), kind=kLoop, calls=%fused_computation | loop fusion | flops 196608 | bytes 264192 | tf_op jit(solution)/shard_map/convert_element_type | solution.py:234
Async XLA Ops:
  0.0 61.0 %copy-start = (f32[512]{0:T(512)S(1)}, f32[512]{0:T(512)}, u32[]{:S(2)}) copy-start(f32[512]{0:T(512)} %param.8) | copy-start | bytes 6148
